TPU v7x, 256 devices: a whole 4x4x8 slice. The times are simulated.
256 devices in a mesh: video: 4 (over z_hi, core), span: 16 (over y, z_lo), head: 4 (over x).
Axes of the slice: x: 4, y: 4, z: 8 (z_hi: 2, z_lo: 4; z = z_hi * 4 + z_lo), core: 2. Of those that a mesh axis runs over, the one named last changes fastest.
Arguments:
- queries: bfloat16 [16384, 48, 128], P(('video', 'span', 'head')), parts along dimension 0, may hold values from -15 to 15
- key_rows: bfloat16 [16384, 48, 128], P(('video', 'span', 'head')), parts along dimension 0, may hold values from -6 to 6
- value_rows: bfloat16 [16384, 48, 128], P(('video', 'span', 'head')), parts along dimension 0, may hold values from -6 to 6
- noise_levels: int32 [64], P('video'), parts along dimension 0, may hold values from 0 to 7
- gate_table: float32 [8, 48], replicated, may hold values from 0.25 to 2
Outputs:
- attended: bfloat16 [16384, 48, 128], P(('video', 'span', 'head')), parts along dimension 0
There are 4 independent parts, one for each index of `video`. A program takes and returns all parts, laid end to end along the dimension named above; an argument that names none is the same for every part. Nothing has to cross between parts.
All inputs are finite; a program needn't handle non-finite values.
Results may differ from a plain program's by a relative error of at most 0.0039.
Values may be sent and summed in bfloat16 or wider, within the bound.
A program may use at most 128 MiB of HBM per device.

v0:
```python
import math

import jax
import jax.numpy as jnp
from jax import lax
from jax.sharding import PartitionSpec as P

BLOCK = 128
LEVELS = 8


def gate_rows_for(noise_levels, gate_table):
    one_hot = (jnp.arange(LEVELS, dtype=jnp.int32)[None, :] == noise_levels[:, None]).astype(
        jnp.float32
    )
    return jnp.dot(one_hot, gate_table, precision=lax.Precision.HIGHEST)


def by_head(queries, key_rows, value_rows, noise_levels, gate_table):
    row_count, head_count, head_width = queries.shape
    head_groups = lax.axis_size("head")
    per_group = head_count // head_groups
    chain_pos = lax.axis_index("span")
    score_scale = 1.0 / math.sqrt(head_width)
    split_shape = (row_count, head_groups, per_group, head_width)
    query_heads, key_heads, value_heads = (
        lax.all_to_all(
            queries.reshape(split_shape), "head", split_axis=1, concat_axis=0, tiled=True
        ),
        lax.all_to_all(
            key_rows.reshape(split_shape), "head", split_axis=1, concat_axis=0, tiled=True
        ),
        lax.all_to_all(
            value_rows.reshape(split_shape), "head", split_axis=1, concat_axis=0, tiled=True
        ),
    )
    span_len = row_count * head_groups
    query_heads = query_heads.reshape(span_len, per_group, head_width)
    key_heads = key_heads.reshape(span_len, per_group, head_width)
    value_heads = value_heads.reshape(span_len, per_group, head_width)
    own_scores = (
        jnp.einsum("qhd,khd->qhk", query_heads, key_heads, preferred_element_type=jnp.float32)
        * score_scale
    )
    query_block = jnp.arange(span_len, dtype=jnp.int32) // BLOCK
    visible = (query_block[None, :] <= query_block[:, None])[:, None, :]
    own_max = jnp.max(jnp.where(visible, own_scores, -jnp.inf), axis=-1)
    own_weights = jnp.where(visible, jnp.exp(own_scores - own_max[..., None]), 0.0)
    own_totals = jnp.sum(own_weights, axis=-1)
    own_acc = jnp.einsum(
        "qhk,khd->qhd",
        own_weights.astype(jnp.bfloat16),
        value_heads,
        preferred_element_type=jnp.float32,
    )
    running = (own_max, own_totals, own_acc)

    def update(state_now, key_block, value_block):
        row_max, totals, accum = state_now
        scores = (
            jnp.einsum("qhd,khd->qhk", query_heads, key_block, preferred_element_type=jnp.float32)
            * score_scale
        )
        new_max = jnp.maximum(row_max, jnp.max(scores, axis=-1))
        rescale = jnp.exp(row_max - new_max)
        weights = jnp.exp(scores - new_max[..., None])
        totals = totals * rescale + jnp.sum(weights, axis=-1)
        accum = accum * rescale[..., None] + jnp.einsum(
            "qhk,khd->qhd",
            weights.astype(jnp.bfloat16),
            value_block,
            preferred_element_type=jnp.float32,
        )
        return (new_max, totals, accum)

    def advance(state_now, inputs):
        key_block, value_block, span_id = inputs
        useful = (span_id >= 0) & (span_id < chain_pos)
        return (
            lax.cond(
                useful,
                lambda inner: update(inner, key_block, value_block),
                lambda inner: inner,
                state_now,
            ),
            None,
        )

    key_piece = lax.all_gather(key_heads, "span", axis=0, tiled=True)
    value_piece = lax.all_gather(value_heads, "span", axis=0, tiled=True)
    block_count = key_piece.shape[0] // span_len
    span_ids = jnp.arange(block_count, dtype=jnp.int32)
    running = lax.scan(
        advance,
        running,
        (
            key_piece.reshape(block_count, span_len, per_group, head_width),
            value_piece.reshape(block_count, span_len, per_group, head_width),
            span_ids,
        ),
    )[0]
    row_max, totals, accum = running
    gate_rows = gate_rows_for(noise_levels, gate_table)
    gate_row = lax.dynamic_index_in_dim(gate_rows, chain_pos, 0, keepdims=False)
    my_gates = lax.dynamic_slice_in_dim(gate_row, lax.axis_index("head") * per_group, per_group, 0)
    result = (accum / totals[..., None] * my_gates[None, :, None]).astype(jnp.bfloat16)
    returned = lax.all_to_all(
        result.reshape(span_len, 1, per_group, head_width),
        "head",
        split_axis=0,
        concat_axis=1,
        tiled=True,
    )
    return returned.reshape(row_count, head_count, head_width)


def body(queries, key_rows, value_rows, noise_levels, gate_table):
    return by_head(queries, key_rows, value_rows, noise_levels, gate_table)


def solution(mesh):
    return jax.shard_map(
        body,
        mesh=mesh,
        in_specs=(
            P(("video", "span", "head"), None, None),
            P(("video", "span", "head"), None, None),
            P(("video", "span", "head"), None, None),
            P("video"),
            P(),
        ),
        out_specs=P(("video", "span", "head"), None, None),
        check_vma=False,
    )
```

profile of v0, /device:TPU:248, one launch (start us, length us, event | category | flops | bytes accessed | tf_op | source)
XLA Modules:
  0.0 706.9 jit_solution(15607178747520992075)
XLA Ops:
  6.5 1.4 copy.38
  8.0 16.4 %all_to_all.60 = bf16[64,4,12,128]{3,0,2,1:T(8,128)(2,1)S(1)} all-to-all(bf16[64,4,12,128]{3,0,2,1:T(8,128)(2,1)S(1)} %bitcast.86), channel_id=1, replica_groups=mesh['video'=4,'span'=16,'head'=4] {'head'}, dimensions={1} | all-to-all | bytes 1572864 | tf_op jit(solution)/shard_map/all_to_all | solution.py:30
  24.3 0.9 copy.39
  25.6 13.8 %all_to_all.61 = bf16[64,4,12,128]{3,0,2,1:T(8,128)(2,1)S(1)} all-to-all(bf16[64,4,12,128]{3,0,2,1:T(8,128)(2,1)S(1)} %bitcast.87), channel_id=1, replica_groups=mesh['video'=4,'span'=16,'head'=4] {'head'}, dimensions={1} | all-to-all | bytes 1572864 | tf_op jit(solution)/shard_map/all_to_all | solution.py:33
  39.4 0.9 copy.43
  40.3 1.1 copy.40
  41.4 3.5 all-to-all-start.1
  45.4 10.0 %all-to-all-done.1 = bf16[64,4,12,128]{3,0,2,1:T(8,128)(2,1)S(1)} async-done(((bf16[64,4,12,128]{3,0,2,1:T(8,128)(2,1)}), bf16[64,4,12,128]{3,0,2,1:T(8,128)(2,1)S(1)}, u32[]{:S(2)}, u32[]{:S(2)}) %all-to-all-start.1) | async-done | bytes 786464 | tf_op jit(solution)/shard_map/all_to_all | solution.py:27
  55.4 0.6 fusion.17
  56.0 0.7 fusion.21
  56.7 1.0 fusion.30
  57.7 236.8 %all-gather.3.cloned.1.call-done = bf16[4096,12,128]{2,0,1:T(8,128)(2,1)} async-done(((bf16[256,12,128]{2,0,1:T(8,128)(2,1)}), bf16[4096,12,128]{2,0,1:T(8,128)(2,1)}) %all-gather.3.cloned.1.call-update) | async-done | bytes 12582928 | tf_op jit(solution)/shard_map/all_gather | solution.py:89
  294.5 11.6 %copy.45 = bf16[16,256,12,128]{3,1,2,0:T(8,128)(2,1)} copy(bf16[16,256,12,128]{3,1,0,2:T(8,128)(2,1)} %bitcast.75) | data formatting | bytes 25165824 | tf_op jit(solution)/shard_map/while | solution.py:93
  306.1 260.5 %all-gather.5.cloned.1.call-done = bf16[4096,12,128]{2,0,1:T(8,128)(2,1)} async-done(((bf16[256,12,128]{2,0,1:T(8,128)(2,1)}), bf16[4096,12,128]{2,0,1:T(8,128)(2,1)}) %all-gather.5.cloned.1.call-update) | async-done | bytes 12582928 | tf_op jit(solution)/shard_map/all_gather | solution.py:90
  566.6 11.6 %copy.46 = bf16[16,256,12,128]{3,1,2,0:T(8,128)(2,1)} copy(bf16[16,256,12,128]{3,1,0,2:T(8,128)(2,1)} %bitcast.76) | data formatting | bytes 25165824 | tf_op jit(solution)/shard_map/while | solution.py:93
  578.2 99.4 %while.14 = (s32[]{:T(128)}, f32[256,12]{0,1:T(8,128)S(1)}, f32[256,12]{0,1:T(8,128)S(1)}, f32[256,12,128]{2,0,1:T(8,128)S(1)}, s32[16]{0:T(128)S(1)}, /*index=5...) while((s32[]{:T(128)}, f32[256,12]{0,1:T(8,128)S(1)}, ...), condition=%wide.region_7.8_spmd, body=%wide.region_2.7_spmd.sunk | while | flops 409737216 | bytes 15140099 | solution.py:93
  580.1 4.6 conditional.2
  580.1 1.7 bitcast_reduce_fusion
  582.4 2.2 bitcast_add_fusion
  586.6 4.6 conditional.2
  586.6 1.7 bitcast_reduce_fusion
  588.9 2.2 bitcast_add_fusion
  593.1 4.6 conditional.2
  593.1 1.7 bitcast_reduce_fusion
  595.4 2.2 bitcast_add_fusion
  599.6 4.6 conditional.2
  599.6 1.7 bitcast_reduce_fusion
  601.9 2.2 bitcast_add_fusion
  606.1 4.6 conditional.2
  606.1 1.7 bitcast_reduce_fusion
  608.5 2.2 bitcast_add_fusion
  612.6 4.6 conditional.2
  612.6 1.7 bitcast_reduce_fusion
  615.0 2.2 bitcast_add_fusion
  619.1 4.6 conditional.2
  619.1 1.7 bitcast_reduce_fusion
  621.5 2.2 bitcast_add_fusion
  625.6 4.6 conditional.2
  625.7 1.7 bitcast_reduce_fusion
  628.0 2.2 bitcast_add_fusion
  632.1 4.6 conditional.2
  632.2 1.7 bitcast_reduce_fusion
  634.5 2.2 bitcast_add_fusion
  638.6 4.6 conditional.2
  638.7 1.7 bitcast_reduce_fusion
  641.0 2.2 bitcast_add_fusion
  645.1 4.6 conditional.2
  645.2 1.7 bitcast_reduce_fusion
  647.5 2.2 bitcast_add_fusion
  651.6 4.6 conditional.2
  651.7 1.7 bitcast_reduce_fusion
  654.0 2.2 bitcast_add_fusion
  658.1 4.6 conditional.2
  658.2 1.7 bitcast_reduce_fusion
  660.5 2.2 bitcast_add_fusion
  664.7 4.6 conditional.2
  664.7 1.7 bitcast_reduce_fusion
  667.0 2.2 bitcast_add_fusion
  671.2 4.6 conditional.2
  671.2 1.7 bitcast_reduce_fusion
  673.5 2.2 bitcast_add_fusion
  677.8 1.4 fusion.33
  679.2 19.1 %all_to_all.62 = bf16[256,1,12,128]{3,2,1,0:T(8,128)(2,1)S(1)} all-to-all(bf16[256,1,12,128]{3,2,1,0:T(8,128)(2,1)S(1)} %fusion.33), channel_id=1, replica_groups=mesh['video'=4,'span'=16,'head'=4] {'head'}, dimensions={0} | all-to-all | bytes 1572864 | tf_op jit(solution)/shard_map/all_to_all | solution.py:107
  698.7 1.4 copy.51
  (105 shorter events, 18.9 us)
Async XLA Ops:
  6.5 38.4 %copy-start = (f32[8,48]{1,0:T(8,128)S(1)}, f32[8,48]{1,0:T(8,128)}, u32[]{:S(2)}) copy-start(f32[8,48]{1,0:T(8,128)} %param.13) | copy-start | bytes 4612
  6.5 18.8 %copy-start.4 = (bf16[64,48,128]{2,1,0:T(8,128)(2,1)S(1)}, bf16[64,48,128]{2,1,0:T(8,128)(2,1)}, u32[]{:S(2)}) copy-start(bf16[64,48,128]{2,1,0:T(8,128)(2,1)} %param.11) | copy-start | bytes 2359300
  6.5 288.0 %all-gather.3.cloned.1.call-start = ((), (), s32[]{:S(2)}) async-start(), calls=%async_computation.4 | async-start | bytes 13369344 | tf_op jit(solution)/shard_map/all_gather | solution.py:89
  25.3 15.1 %copy-start.5 = (bf16[64,48,128]{2,1,0:T(8,128)(2,1)S(1)}, bf16[64,48,128]{2,1,0:T(8,128)(2,1)}, u32[]{:S(2)}) copy-start(bf16[64,48,128]{2,1,0:T(8,128)(2,1)} %param.9) | copy-start | bytes 2359300
  25.3 541.3 %all-gather.5.cloned.1.call-start = ((), (), s32[]{:S(2)}) async-start(), calls=%async_computation.5 | async-start | bytes 13369344 | tf_op jit(solution)/shard_map/all_gather | solution.py:90
  39.4 5.6 copy-start.6
  40.3 15.1 %copy-start.2 = (bf16[4,64,1,12,128]{4,1,0,3,2:T(8,128)(2,1)S(1)}, bf16[4,64,1,12,128]{4,1,0,3,2:T(8,128)(2,1)}, u32[]{:S(2)}) copy-start(bf16[4,64,1,12,128]{4,1,0,3,2:T(8,128)(2,1)} %copy.39) | copy-start | bytes 2359300
  41.4 13.9 %all-to-all-start.1 = ((bf16[64,4,12,128]{3,0,2,1:T(8,128)(2,1)}), bf16[64,4,12,128]{3,0,2,1:T(8,128)(2,1)S(1)}, u32[]{:S(2)}, u32[]{:S(2)}) async-start(bf16[64,4,12,128]{3,0,2,1:T(8,128)(2,1)} %bitcast.9), calls=%async_computation.1 | async-start | bytes 1572864 | tf_op jit(solution)/shard_map/all_to_all | solution.py:27
  55.4 1.3 copy-start.3
  677.8 22.2 %copy-start.1 = (f32[8,48]{1,0:T(8,128)S(1)}, f32[8,48]{1,0:T(8,128)}, u32[]{:S(2)}) copy-start(f32[8,48]{1,0:T(8,128)} %param.13) | copy-start | bytes 4612
Sparse Core Ops, SparseCore 0:
  25.4 269.0 all-gather.2
  296.3 270.2 all-gather.4
where the time goes:
time: 709 us; the launch traced here: 707 us
  waiting for transfers between devices  507 us (72%)
  matrix products  61.3 us (9%)
  blocking collectives  49.3 us (7%)
  local copies, waits for them, and re-layouts  39.2 us (6%)
  loops' own time  22.1 us (3%)
  between operations  13.6 us (2%)
  other arithmetic  10.6 us (1%)
    all_gather x1, waiting for transfers between devices, by_head(): value_piece = lax.all_gather(value_heads, 'span', axis=0, tiled=True)  260 us
    all_gather x1, waiting for transfers between devices, by_head(): key_piece = lax.all_gather(key_heads, 'span', axis=0, tiled=True)  237 us
    dot_general x15, matrix products, update(): jnp.einsum('qhk,khd->qhd', weights.astype(jnp.bfloat16), value_block, pre...  33.7 us
    dot_general x15, matrix products, update(): jnp.einsum('qhd,khd->qhk', query_heads, key_block, preferred_element_type...  25.9 us
    while x3, local copies, waits for them, and re-layouts, by_head(): lax.scan(advance, running, (key_piece.reshape(block_count, span_len, per_...  23.4 us
    another operation x1, loops' own time, by_head(): lax.scan(advance, running, (key_piece.reshape(block_count, span_len, per_...  21.2 us
    all_to_all x1, blocking collectives, by_head(): lax.all_to_all(result.reshape(span_len, 1, per_group, head_width), 'head'...  19.1 us
    all_to_all x1, blocking collectives, by_head(): lax.all_to_all(key_rows.reshape(split_shape), 'head', split_axis=1, conca...  16.4 us
  transfers between devices with their start and end apart: 3, of which 3 were waited for; matrix products, arithmetic and copies ran while one was open for 2% of the time, Pallas kernels for 0%

commit v1 on v0

v1 whole, which is shorter than its diff:
```python
import functools
import math

import jax
import jax.numpy as jnp
from jax import lax
from jax.experimental import pallas as pl
from jax.experimental.pallas import tpu as pltpu
from jax.sharding import PartitionSpec as P

MESH = pl.DeviceIdType.MESH
HEADS = 48
DIM = 128
ROWS = 64
SPANS = 16
QUARTERS = 4
SPAN = ROWS * QUARTERS
PEERS = SPANS * QUARTERS
GROUP = 4
CHUNK = SPAN * GROUP
CHUNKS = SPANS // GROUP
BLOCK = 128
HIDDEN = -1e30
SCALE = math.log2(math.e) / math.sqrt(DIM)


def pair_index(span, chunk):
    group = span // GROUP
    return 2 * group * (group + 1) + (span % GROUP) * (group + 1) + chunk


PAIRS = 2 * CHUNKS * (CHUNKS + 1)


def kernel(
    queries, key_rows, value_rows, noise_levels, gate_table, out,
    wide, send_qk, send_v, got_qk, got_v, scores, weights, totals, send_o, got_o,
    qk_sent, qk_here, v_sent, v_here, o_sent, o_here, own_qk, own_v,
):
    core = lax.axis_index("video") % 2
    span = lax.axis_index("span")
    x = lax.axis_index("head")
    y = span // 4
    z = span % 4
    me = span * QUARTERS + x

    def place(column_x, column_y, j):
        z_at = (0, 1 + core, 3)[j]
        return (column_y * 4 + column_x) * 3 + j, column_y * 4 + z_at, column_x

    active = (z == 0) | (z == 3) | (z == 1 + core)
    j_mine = jnp.where(z == 0, 0, jnp.where(z == 3, 2, 1))
    my_head = (y * 4 + x) * 3 + j_mine

    barrier = pltpu.get_barrier_semaphore()

    def greet(i, carry):
        other = lax.rem(me + i, PEERS)
        pl.semaphore_signal(
            barrier,
            inc=1,
            device_id={"span": other // QUARTERS, "head": other % QUARTERS},
            device_id_type=MESH,
        )
        return carry

    lax.fori_loop(1, PEERS, greet, 0)

    def by_head(ref, store):
        wide[...] = ref[...].reshape(ROWS * HEADS, DIM).astype(jnp.float32)

        def one(h, carry):
            store(h, wide[pl.ds(h, ROWS, stride=HEADS), :].astype(jnp.bfloat16))
            return carry

        lax.fori_loop(0, HEADS, one, 0)

    def store_q(h, rows):
        send_qk[h, 0] = rows

    def store_k(h, rows):
        send_qk[h, 1] = rows

    def store_v(h, rows):
        send_v[h] = rows

    by_head(queries, store_q)
    by_head(key_rows, store_k)
    pl.semaphore_wait(barrier, PEERS - 1)

    def scatter(source, target, sent, here, own):
        def column(k, carry):
            column_x = lax.rem(x + k % 4, 4)
            column_y = lax.rem(y + k // 4, 4)
            for j in range(3):
                head, to_span, to_x = place(column_x, column_y, j)
                mine = (to_span == span) & (to_x == x)

                @pl.when(jnp.logical_not(mine))
                def _():
                    pltpu.make_async_remote_copy(
                        source.at[head],
                        target.at[me],
                        sent,
                        here,
                        device_id={"span": to_span, "head": to_x},
                        device_id_type=MESH,
                    ).start()

                @pl.when(mine)
                def _():
                    pltpu.make_async_copy(source.at[head], target.at[me], own).start()

            return carry

        lax.fori_loop(0, 16, column, 0)

    scatter(send_qk, got_qk, qk_sent, qk_here, own_qk)
    by_head(value_rows, store_v)
    scatter(send_v, got_v, v_sent, v_here, own_v)

    def wait_for(ref, count, semaphore):
        part = ref.at[pl.ds(0, count)]
        pltpu.make_async_copy(part, part, semaphore).wait()

    @pl.when(active)
    def _():
        wait_for(got_qk, PEERS - 1, qk_here)
        wait_for(got_qk, 1, own_qk)

        def soften(i, carry):
            group = i // GROUP
            place_in_group = i % GROUP
            q = got_qk[pl.ds(i * QUARTERS, QUARTERS), 0].reshape(SPAN, DIM)

            def raw(c):
                keys = got_qk[pl.ds(c * (GROUP * QUARTERS), GROUP * QUARTERS), 1]
                return lax.dot_general(
                    q,
                    keys.reshape(CHUNK, DIM),
                    (((1,), (1,)), ((), ())),
                    preferred_element_type=jnp.float32,
                )

            def lanes(value, op):
                parts = [value[:, k * BLOCK : (k + 1) * BLOCK] for k in range(CHUNK // BLOCK)]
                while len(parts) > 1:
                    parts = [op(a, b) for a, b in zip(parts[::2], parts[1::2])]
                return parts[0]

            s = raw(group)
            columns = []
            for k in range(CHUNK // BLOCK):
                halves = []
                for half in range(SPAN // BLOCK):
                    block = s[half * BLOCK : (half + 1) * BLOCK, k * BLOCK : (k + 1) * BLOCK]
                    seen = k <= 2 * place_in_group + half
                    halves.append(jnp.where(seen, block, HIDDEN))
                columns.append(jnp.concatenate(halves, axis=0))
            s = jnp.concatenate(columns, axis=1)
            scores[group] = s
            top = lanes(s, jnp.maximum)

            def full(c, top):
                s = raw(c)
                scores[c] = s
                return jnp.maximum(top, lanes(s, jnp.maximum))

            top = lax.fori_loop(0, group, full, top)
            row_max = jnp.max(top, axis=1, keepdims=True)

            def weigh(c, total):
                w = jnp.exp2((scores[c] - row_max) * SCALE)
                weights[pair_index(i, c)] = w.astype(jnp.bfloat16)
                return total + lanes(w, jnp.add)

            total = lax.fori_loop(0, group + 1, weigh, jnp.zeros((SPAN, BLOCK), jnp.float32))
            totals[i] = jnp.sum(total, axis=1, keepdims=True)
            return carry

        lax.fori_loop(0, SPANS, soften, 0)

        wait_for(got_v, PEERS - 1, v_here)
        wait_for(got_v, 1, own_v)

        def gather(i, carry):
            def add(c, acc):
                values = got_v[pl.ds(c * (GROUP * QUARTERS), GROUP * QUARTERS)]
                return acc + jnp.dot(
                    weights[pair_index(i, c)],
                    values.reshape(CHUNK, DIM),
                    preferred_element_type=jnp.float32,
                )

            acc = lax.fori_loop(0, i // GROUP + 1, add, jnp.zeros((SPAN, DIM), jnp.float32))
            gate = gate_table[noise_levels[i], my_head]
            result = (acc / totals[i] * gate).astype(jnp.bfloat16)
            send_o[pl.ds(i * QUARTERS, QUARTERS)] = result.reshape(QUARTERS, ROWS, DIM)
            for quarter in range(QUARTERS):
                piece = i * QUARTERS + quarter
                mine = piece == me

                @pl.when(jnp.logical_not(mine))
                def _():
                    pltpu.make_async_remote_copy(
                        send_o.at[piece],
                        got_o.at[my_head],
                        o_sent,
                        o_here,
                        device_id={"span": i, "head": quarter},
                        device_id_type=MESH,
                    ).start()

                @pl.when(mine)
                def _():
                    got_o[my_head] = send_o[piece]

            return carry

        lax.fori_loop(0, SPANS, gather, 0)
        wait_for(got_o, HEADS - 1, o_here)
        wait_for(send_qk, HEADS - 1, qk_sent)
        wait_for(send_v, HEADS - 1, v_sent)
        wait_for(send_o, PEERS - 1, o_sent)

    @pl.when(jnp.logical_not(active))
    def _():
        wait_for(got_o, HEADS, o_here)
        wait_for(send_qk, HEADS, qk_sent)
        wait_for(send_v, HEADS, v_sent)

    wide[...] = got_o[...].reshape(HEADS * ROWS, DIM).astype(jnp.float32)

    def token(t, carry):
        out[t] = wide[pl.ds(t, HEADS, stride=ROWS), :].astype(jnp.bfloat16)
        return carry

    lax.fori_loop(0, ROWS, token, 0)


def body(queries, key_rows, value_rows, noise_levels, gate_table):
    vmem = pl.BlockSpec(memory_space=pltpu.VMEM)
    smem = pl.BlockSpec(memory_space=pltpu.SMEM)
    bf16, f32 = jnp.bfloat16, jnp.float32
    return pl.pallas_call(
        kernel,
        out_shape=jax.ShapeDtypeStruct((ROWS, HEADS, DIM), bf16),
        in_specs=[vmem, vmem, vmem, smem, smem],
        out_specs=vmem,
        scratch_shapes=[
            pltpu.VMEM((ROWS * HEADS, DIM), f32),
            pltpu.VMEM((HEADS, 2, ROWS, DIM), bf16),
            pltpu.VMEM((HEADS, ROWS, DIM), bf16),
            pltpu.VMEM((PEERS, 2, ROWS, DIM), bf16),
            pltpu.VMEM((PEERS, ROWS, DIM), bf16),
            pltpu.VMEM((CHUNKS, SPAN, CHUNK), f32),
            pltpu.VMEM((PAIRS, SPAN, CHUNK), bf16),
            pltpu.VMEM((SPANS, SPAN, 1), f32),
            pltpu.VMEM((PEERS, ROWS, DIM), bf16),
            pltpu.VMEM((HEADS, ROWS, DIM), bf16),
        ]
        + [pltpu.SemaphoreType.DMA] * 8,
        compiler_params=pltpu.CompilerParams(
            collective_id=0, has_side_effects=True, vmem_limit_bytes=56 << 20
        ),
    )(queries, key_rows, value_rows, noise_levels, gate_table)


def solution(mesh):
    return jax.shard_map(
        body,
        mesh=mesh,
        in_specs=(
            P(("video", "span", "head"), None, None),
            P(("video", "span", "head"), None, None),
            P(("video", "span", "head"), None, None),
            P("video"),
            P(),
        ),
        out_specs=P(("video", "span", "head"), None, None),
        check_vma=False,
    )
```

time: 709 us -> 104 us (0.15)
  waiting for transfers between devices: 507 us -> 0 us
  Pallas kernels: 0 us -> 102 us
  matrix products: 61.3 us -> 0 us
  blocking collectives: 49.3 us -> 0 us
  local copies, waits for them, and re-layouts: 39.2 us -> 2.06 us
  loops' own time: 22.1 us -> 0 us
  between operations: 13.6 us -> 0.01 us
  other arithmetic: 10.6 us -> 0 us
    all_gather x2 -> x0, waiting for transfers between devices: 497 us -> none  [the longest x1 260 us: by_head(): value_piece = lax.all_gather(value_heads, 'span', axis=0, tiled=True)]
    pallas_call x0 -> x1, Pallas kernels: none -> 102 us  [body(): pl.pallas_call(kernel, out_shape=jax.ShapeDtypeStruct((ROWS, HEADS, DIM),...]
    dot_general x33 -> x0, matrix products: 61.3 us -> none  [the longest x15 33.7 us: update(): jnp.einsum('qhk,khd->qhd', weights.astype(jnp.bfloat16), value_block, pre...]
    all_to_all x3 -> x0, blocking collectives: 49.3 us -> none  [the longest x1 19.1 us: by_head(): lax.all_to_all(result.reshape(span_len, 1, per_group, head_width), 'head'...]
    while x3 -> x0, local copies, waits for them, and re-layouts: 23.4 us -> none  [by_head(): lax.scan(advance, running, (key_piece.reshape(block_count, span_len, per_...]
    another operation x17 -> x0, loops' own time: 22.1 us -> none  [the longest x1 21.2 us: by_head(): lax.scan(advance, running, (key_piece.reshape(block_count, span_len, per_...]
    all_to_all x1 -> x0, waiting for transfers between devices: 9.99 us -> none  [by_head(): lax.all_to_all(queries.reshape(split_shape), 'head', split_axis=1, concat...]
    dynamic_slice x16 -> x0, local copies, waits for them, and re-layouts: 9.39 us -> none  [by_head(): lax.scan(advance, running, (key_piece.reshape(block_count, span_len, per_...]
  transfers between devices with their start and end apart: 3 -> 0, of which waited for: 3 -> 0; matrix products, arithmetic and copies ran while one was open for 2% -> 0% of each run, Pallas kernels for 0% -> 0%
where the time goes in v1:
time: 104 us
  Pallas kernels  102 us (98%)
  local copies, waits for them, and re-layouts  2.06 us (2%)
    pallas_call x1, Pallas kernels, body(): pl.pallas_call(kernel, out_shape=jax.ShapeDtypeStruct((ROWS, HEADS, DIM),...  102 us

profile of v1, /device:TPU:248, one launch (start us, length us, event | category | flops | bytes accessed | tf_op | source)
XLA Modules:
  0.0 104.0 jit_solution(5457220447004508277)
XLA Ops:
  0.0 101.9 %shard_map.55 = bf16[64,48,128]{2,1,0:T(8,128)(2,1)} custom-call(bf16[64,48,128]{2,1,0:T(8,128)(2,1)} %queries.1, bf16[64,48,128]{2,1,0:T(8,128)(2,1)} %key_rows.1, bf16[64,48,128]{2,1,0:T(8,128)(2,1)} %value_rows.1, s32[16]{0:T(128)} %noise_levels.1, f32[8,48]{1,0:T(8,128)} %gate_table.1), custom_call_target="tpu_custom_call" | custom-call | tf_op jit(solution)/shard_map/pallas_call | solution.py:245
  102.0 2.1 %copy.7 = bf16[64,48,128]{2,1,0:T(8,128)(2,1)} copy(bf16[64,48,128]{2,1,0:T(8,128)(2,1)} %shard_map.55) | data formatting | bytes 1572864

commit v2 on v1

--- a/solution.py
+++ b/solution.py
@@ -22,19 +22,32 @@
 BLOCK = 128
 HIDDEN = -1e30
 SCALE = math.log2(math.e) / math.sqrt(DIM)
-
-
-def pair_index(span, chunk):
-    group = span // GROUP
-    return 2 * group * (group + 1) + (span % GROUP) * (group + 1) + chunk
-
-
-PAIRS = 2 * CHUNKS * (CHUNKS + 1)
+PAIRS = CHUNKS * (CHUNKS + 1) // 2
+
+
+def pair_at(group, chunk):
+    return group * (group + 1) // 2 + chunk
+
+
+def raw_scores(q, keys):
+    return lax.dot_general(q, keys, (((1,), (1,)), ((), ())), preferred_element_type=jnp.float32)
+
+
+def blocks_of(value):
+    return [value[:, k * BLOCK : (k + 1) * BLOCK] for k in range(value.shape[1] // BLOCK)]
+
+
+def fold(parts, op):
+    parts = list(parts)
+    while len(parts) > 1:
+        paired = [op(left, right) for left, right in zip(parts[::2], parts[1::2])]
+        parts = paired + (parts[-1:] if len(parts) % 2 else [])
+    return parts[0]
 
 
 def kernel(
     queries, key_rows, value_rows, noise_levels, gate_table, out,
-    wide, send_qk, send_v, got_qk, got_v, scores, weights, totals, send_o, got_o,
+    wide, send_qk, send_v, got_qk, got_v, weights, peaks, tops, shares, sums, acc, send_o, got_o,
     qk_sent, qk_here, v_sent, v_here, o_sent, o_here, own_qk, own_v,
 ):
     core = lax.axis_index("video") % 2
@@ -128,96 +141,102 @@
         wait_for(got_qk, PEERS - 1, qk_here)
         wait_for(got_qk, 1, own_qk)
 
-        def soften(i, carry):
-            group = i // GROUP
-            place_in_group = i % GROUP
-            q = got_qk[pl.ds(i * QUARTERS, QUARTERS), 0].reshape(SPAN, DIM)
-
-            def raw(c):
-                keys = got_qk[pl.ds(c * (GROUP * QUARTERS), GROUP * QUARTERS), 1]
-                return lax.dot_general(
-                    q,
-                    keys.reshape(CHUNK, DIM),
-                    (((1,), (1,)), ((), ())),
+        def q_of(group, r):
+            return got_qk[pl.ds((group * GROUP + r) * QUARTERS, QUARTERS), 0].reshape(SPAN, DIM)
+
+        def keys_of(chunk, spans):
+            first = chunk * (GROUP * QUARTERS)
+            return got_qk[pl.ds(first, spans * QUARTERS), 1].reshape(spans * SPAN, DIM)
+
+        def values_of(chunk, spans):
+            first = chunk * (GROUP * QUARTERS)
+            return got_v[pl.ds(first, spans * QUARTERS)].reshape(spans * SPAN, DIM)
+
+        def weigh(pair, r, columns, top):
+            ws = [jnp.exp2((s - top) * SCALE) for s in columns]
+            for k, w in enumerate(ws):
+                weights[pair, r, :, k * BLOCK : (k + 1) * BLOCK] = w.astype(jnp.bfloat16)
+            peaks[pair, r] = top
+            return fold(ws, jnp.add)
+
+        def soften(group, carry):
+            for r in range(GROUP):
+                columns = blocks_of(raw_scores(q_of(group, r), keys_of(group, r + 1)))
+                hidden = jnp.full((BLOCK, BLOCK), HIDDEN, jnp.float32)
+                columns[-1] = jnp.concatenate([hidden, columns[-1][BLOCK:]], axis=0)
+                top = jnp.max(fold(columns, jnp.maximum), axis=1, keepdims=True)
+                sums[r] = weigh(pair_at(group, group), r, columns, top)
+                tops[group, r] = top
+
+            def earlier(chunk, carry):
+                for r in range(GROUP):
+                    columns = blocks_of(raw_scores(q_of(group, r), keys_of(chunk, GROUP)))
+                    before = tops[group, r]
+                    top = jnp.max(fold(columns, jnp.maximum), axis=1, keepdims=True)
+                    top = jnp.maximum(before, top)
+                    added = weigh(pair_at(group, chunk), r, columns, top)
+                    sums[r] = sums[r] * jnp.exp2((before - top) * SCALE) + added
+                    tops[group, r] = top
+                return carry
+
+            lax.fori_loop(0, group, earlier, 0)
+            for r in range(GROUP):
+                gate = gate_table[noise_levels[group * GROUP + r], my_head]
+                shares[group, r] = gate / jnp.sum(sums[r], axis=1, keepdims=True)
+            return carry
+
+        lax.fori_loop(0, CHUNKS, soften, 0)
+
+        wait_for(got_v, PEERS - 1, v_here)
+        wait_for(got_v, 1, own_v)
+
+        def gather(step, carry):
+            group = step
+
+            def term(chunk, spans, r):
+                pair = pair_at(group, chunk)
+                rescale = jnp.exp2((peaks[pair, r] - tops[group, r]) * SCALE)
+                return rescale * jnp.dot(
+                    weights[pair, r, :, 0 : spans * SPAN],
+                    values_of(chunk, spans),
                     preferred_element_type=jnp.float32,
                 )
 
-            def lanes(value, op):
-                parts = [value[:, k * BLOCK : (k + 1) * BLOCK] for k in range(CHUNK // BLOCK)]
-                while len(parts) > 1:
-                    parts = [op(a, b) for a, b in zip(parts[::2], parts[1::2])]
-                return parts[0]
-
-            s = raw(group)
-            columns = []
-            for k in range(CHUNK // BLOCK):
-                halves = []
-                for half in range(SPAN // BLOCK):
-                    block = s[half * BLOCK : (half + 1) * BLOCK, k * BLOCK : (k + 1) * BLOCK]
-                    seen = k <= 2 * place_in_group + half
-                    halves.append(jnp.where(seen, block, HIDDEN))
-                columns.append(jnp.concatenate(halves, axis=0))
-            s = jnp.concatenate(columns, axis=1)
-            scores[group] = s
-            top = lanes(s, jnp.maximum)
-
-            def full(c, top):
-                s = raw(c)
-                scores[c] = s
-                return jnp.maximum(top, lanes(s, jnp.maximum))
-
-            top = lax.fori_loop(0, group, full, top)
-            row_max = jnp.max(top, axis=1, keepdims=True)
-
-            def weigh(c, total):
-                w = jnp.exp2((scores[c] - row_max) * SCALE)
-                weights[pair_index(i, c)] = w.astype(jnp.bfloat16)
-                return total + lanes(w, jnp.add)
-
-            total = lax.fori_loop(0, group + 1, weigh, jnp.zeros((SPAN, BLOCK), jnp.float32))
-            totals[i] = jnp.sum(total, axis=1, keepdims=True)
+            for r in range(GROUP):
+                acc[r] = term(group, r + 1, r)
+
+            def earlier(chunk, carry):
+                for r in range(GROUP):
+                    acc[r] += term(chunk, GROUP, r)
+                return carry
+
+            lax.fori_loop(0, group, earlier, 0)
+            for r in range(GROUP):
+                i = group * GROUP + r
+                result = (acc[r] * shares[group, r]).astype(jnp.bfloat16)
+                send_o[pl.ds(i * QUARTERS, QUARTERS)] = result.reshape(QUARTERS, ROWS, DIM)
+                for quarter in range(QUARTERS):
+                    piece = i * QUARTERS + quarter
+                    mine = piece == me
+
+                    @pl.when(jnp.logical_not(mine))
+                    def _():
+                        pltpu.make_async_remote_copy(
+                            send_o.at[piece],
+                            got_o.at[my_head],
+                            o_sent,
+                            o_here,
+                            device_id={"span": i, "head": quarter},
+                            device_id_type=MESH,
+                        ).start()
+
+                    @pl.when(mine)
+                    def _():
+                        got_o[my_head] = send_o[piece]
+
             return carry
 
-        lax.fori_loop(0, SPANS, soften, 0)
-
-        wait_for(got_v, PEERS - 1, v_here)
-        wait_for(got_v, 1, own_v)
-
-        def gather(i, carry):
-            def add(c, acc):
-                values = got_v[pl.ds(c * (GROUP * QUARTERS), GROUP * QUARTERS)]
-                return acc + jnp.dot(
-                    weights[pair_index(i, c)],
-                    values.reshape(CHUNK, DIM),
-                    preferred_element_type=jnp.float32,
-                )
-
-            acc = lax.fori_loop(0, i // GROUP + 1, add, jnp.zeros((SPAN, DIM), jnp.float32))
-            gate = gate_table[noise_levels[i], my_head]
-            result = (acc / totals[i] * gate).astype(jnp.bfloat16)
-            send_o[pl.ds(i * QUARTERS, QUARTERS)] = result.reshape(QUARTERS, ROWS, DIM)
-            for quarter in range(QUARTERS):
-                piece = i * QUARTERS + quarter
-                mine = piece == me
-
-                @pl.when(jnp.logical_not(mine))
-                def _():
-                    pltpu.make_async_remote_copy(
-                        send_o.at[piece],
-                        got_o.at[my_head],
-                        o_sent,
-                        o_here,
-                        device_id={"span": i, "head": quarter},
-                        device_id_type=MESH,
-                    ).start()
-
-                @pl.when(mine)
-                def _():
-                    got_o[my_head] = send_o[piece]
-
-            return carry
-
-        lax.fori_loop(0, SPANS, gather, 0)
+        lax.fori_loop(0, CHUNKS, gather, 0)
         wait_for(got_o, HEADS - 1, o_here)
         wait_for(send_qk, HEADS - 1, qk_sent)
         wait_for(send_v, HEADS - 1, v_sent)
@@ -253,9 +272,12 @@
             pltpu.VMEM((HEADS, ROWS, DIM), bf16),
             pltpu.VMEM((PEERS, 2, ROWS, DIM), bf16),
             pltpu.VMEM((PEERS, ROWS, DIM), bf16),
-            pltpu.VMEM((CHUNKS, SPAN, CHUNK), f32),
-            pltpu.VMEM((PAIRS, SPAN, CHUNK), bf16),
-            pltpu.VMEM((SPANS, SPAN, 1), f32),
+            pltpu.VMEM((PAIRS, GROUP, SPAN, CHUNK), bf16),
+            pltpu.VMEM((PAIRS, GROUP, SPAN, 1), f32),
+            pltpu.VMEM((CHUNKS, GROUP, SPAN, 1), f32),
+            pltpu.VMEM((CHUNKS, GROUP, SPAN, 1), f32),
+            pltpu.VMEM((GROUP, SPAN, BLOCK), f32),
+            pltpu.VMEM((GROUP, SPAN, DIM), f32),
             pltpu.VMEM((PEERS, ROWS, DIM), bf16),
             pltpu.VMEM((HEADS, ROWS, DIM), bf16),
         ]

time: 104 us -> 92.8 us (0.89); the launches traced: 104 us -> 91 us
  Pallas kernels: 102 us -> 89 us
    pallas_call x1, Pallas kernels: 102 us -> 89 us  [body(): pl.pallas_call(kernel, out_shape=jax.ShapeDtypeStruct((ROWS, HEADS, DIM),...]
where the time goes in v2:
time: 92.8 us; the launch traced here: 91 us
  Pallas kernels  89 us (96%)
  local copies, waits for them, and re-layouts  2.06 us (2%)
    pallas_call x1, Pallas kernels, body(): pl.pallas_call(kernel, out_shape=jax.ShapeDtypeStruct((ROWS, HEADS, DIM),...  89 us
    unnamed x1, local copies, waits for them, and re-layouts  2.06 us

profile of v2, /device:TPU:248, one launch (start us, length us, event | category | flops | bytes accessed | tf_op | source)
XLA Modules:
  0.0 91.0 jit_solution(12502233818088767190)
XLA Ops:
  0.0 89.0 %shard_map.55 = bf16[64,48,128]{2,1,0:T(8,128)(2,1)} custom-call(bf16[64,48,128]{2,1,0:T(8,128)(2,1)} %queries.1, bf16[64,48,128]{2,1,0:T(8,128)(2,1)} %key_rows.1, bf16[64,48,128]{2,1,0:T(8,128)(2,1)} %value_rows.1, s32[16]{0:T(128)} %noise_levels.1, f32[8,48]{1,0:T(8,128)} %gate_table.1), custom_call_target="tpu_custom_call" | custom-call | tf_op jit(solution)/shard_map/pallas_call | solution.py:264
  89.0 2.1 %copy.7 = bf16[64,48,128]{2,1,0:T(8,128)(2,1)} copy(bf16[64,48,128]{2,1,0:T(8,128)(2,1)} %shard_map.55) | data formatting | bytes 1572864

commit v3 on v2

--- a/solution.py
+++ b/solution.py
@@ -46,9 +46,9 @@
 
 
 def kernel(
-    queries, key_rows, value_rows, noise_levels, gate_table, out,
-    wide, send_qk, send_v, got_qk, got_v, weights, peaks, tops, shares, sums, acc, send_o, got_o,
-    qk_sent, qk_here, v_sent, v_here, o_sent, o_here, own_qk, own_v,
+    queries_hbm, key_rows_hbm, value_rows_hbm, noise_levels, gate_table, out,
+    queries, key_rows, value_rows, loaded, wide, send_qk, send_v, got_qk, got_v, weights, peaks, tops, shares, sums, acc, send_o, got_o,
+    qk_sent, qk_here, v_sent, v_here, o_sent, o_here, own_qk, own_v, plane_in,
 ):
     core = lax.axis_index("video") % 2
     span = lax.axis_index("span")
@@ -65,19 +65,32 @@
     j_mine = jnp.where(z == 0, 0, jnp.where(z == 3, 2, 1))
     my_head = (y * 4 + x) * 3 + j_mine
 
+    loads = [
+        pltpu.make_async_copy(source, target, loaded.at[n])
+        for n, (source, target) in enumerate(
+            [(queries_hbm, queries), (key_rows_hbm, key_rows), (value_rows_hbm, value_rows)]
+        )
+    ]
+    for load in loads:
+        load.start()
+
     barrier = pltpu.get_barrier_semaphore()
 
-    def greet(i, carry):
-        other = lax.rem(me + i, PEERS)
+    def signal(semaphore, to_span, to_x):
         pl.semaphore_signal(
-            barrier,
+            semaphore,
             inc=1,
-            device_id={"span": other // QUARTERS, "head": other % QUARTERS},
+            device_id={"span": to_span, "head": to_x},
             device_id_type=MESH,
         )
-        return carry
-
-    lax.fori_loop(1, PEERS, greet, 0)
+
+    def greet_column(semaphore):
+        for i in range(1, 4):
+            signal(semaphore, y * 4 + lax.rem(z + i, 4), x)
+
+    greet_column(barrier)
+    for i in range(1, 16):
+        signal(barrier, lax.rem(y + i // 4, 4) * 4 + z, lax.rem(x + i % 4, 4))
 
     def by_head(ref, store):
         wide[...] = ref[...].reshape(ROWS * HEADS, DIM).astype(jnp.float32)
@@ -97,11 +110,14 @@
     def store_v(h, rows):
         send_v[h] = rows
 
+    loads[0].wait()
     by_head(queries, store_q)
+    loads[1].wait()
     by_head(key_rows, store_k)
-    pl.semaphore_wait(barrier, PEERS - 1)
-
-    def scatter(source, target, sent, here, own):
+    pl.semaphore_wait(barrier, 3 + 15)
+    greet_column(plane_in)
+
+    def scatter(first, last, source, target, sent, here, own):
         def column(k, carry):
             column_x = lax.rem(x + k % 4, 4)
             column_y = lax.rem(y + k // 4, 4)
@@ -126,11 +142,14 @@
 
             return carry
 
-        lax.fori_loop(0, 16, column, 0)
-
-    scatter(send_qk, got_qk, qk_sent, qk_here, own_qk)
+        lax.fori_loop(first, last, column, 0)
+
+    scatter(0, 1, send_qk, got_qk, qk_sent, qk_here.at[y], own_qk)
+    pl.semaphore_wait(plane_in, 3)
+    scatter(1, 16, send_qk, got_qk, qk_sent, qk_here.at[y], own_qk)
+    loads[2].wait()
     by_head(value_rows, store_v)
-    scatter(send_v, got_v, v_sent, v_here, own_v)
+    scatter(0, 16, send_v, got_v, v_sent, v_here, own_v)
 
     def wait_for(ref, count, semaphore):
         part = ref.at[pl.ds(0, count)]
@@ -138,9 +157,6 @@
 
     @pl.when(active)
     def _():
-        wait_for(got_qk, PEERS - 1, qk_here)
-        wait_for(got_qk, 1, own_qk)
-
         def q_of(group, r):
             return got_qk[pl.ds((group * GROUP + r) * QUARTERS, QUARTERS), 0].reshape(SPAN, DIM)
 
@@ -159,33 +175,59 @@
             peaks[pair, r] = top
             return fold(ws, jnp.add)
 
-        def soften(group, carry):
+        def own_chunk(group):
             for r in range(GROUP):
                 columns = blocks_of(raw_scores(q_of(group, r), keys_of(group, r + 1)))
                 hidden = jnp.full((BLOCK, BLOCK), HIDDEN, jnp.float32)
                 columns[-1] = jnp.concatenate([hidden, columns[-1][BLOCK:]], axis=0)
                 top = jnp.max(fold(columns, jnp.maximum), axis=1, keepdims=True)
-                sums[r] = weigh(pair_at(group, group), r, columns, top)
+                sums[group, r] = weigh(pair_at(group, group), r, columns, top)
                 tops[group, r] = top
 
-            def earlier(chunk, carry):
-                for r in range(GROUP):
-                    columns = blocks_of(raw_scores(q_of(group, r), keys_of(chunk, GROUP)))
-                    before = tops[group, r]
-                    top = jnp.max(fold(columns, jnp.maximum), axis=1, keepdims=True)
-                    top = jnp.maximum(before, top)
-                    added = weigh(pair_at(group, chunk), r, columns, top)
-                    sums[r] = sums[r] * jnp.exp2((before - top) * SCALE) + added
-                    tops[group, r] = top
+        def earlier_chunk(group, chunk):
+            for r in range(GROUP):
+                columns = blocks_of(raw_scores(q_of(group, r), keys_of(chunk, GROUP)))
+                before = tops[group, r]
+                top = jnp.max(fold(columns, jnp.maximum), axis=1, keepdims=True)
+                top = jnp.maximum(before, top)
+                added = weigh(pair_at(group, chunk), r, columns, top)
+                sums[group, r] = sums[group, r] * jnp.exp2((before - top) * SCALE) + added
+                tops[group, r] = top
+
+        def row_of(step):
+            return lax.rem(y + CHUNKS - step, CHUNKS)
+
+        def soften(step, carry):
+            row = row_of(step)
+
+            @pl.when(step == 0)
+            def _():
+                wait_for(got_qk, 15, qk_here.at[row])
+                wait_for(got_qk, 1, own_qk)
+
+            @pl.when(step > 0)
+            def _():
+                wait_for(got_qk, 16, qk_here.at[row])
+
+            own_chunk(row)
+
+            def with_row(before, carry):
+                other = row_of(before)
+                earlier_chunk(jnp.maximum(row, other), jnp.minimum(row, other))
                 return carry
 
-            lax.fori_loop(0, group, earlier, 0)
+            lax.fori_loop(0, step, with_row, 0)
+            return carry
+
+        lax.fori_loop(0, CHUNKS, soften, 0)
+
+        def share(group, carry):
             for r in range(GROUP):
                 gate = gate_table[noise_levels[group * GROUP + r], my_head]
-                shares[group, r] = gate / jnp.sum(sums[r], axis=1, keepdims=True)
-            return carry
-
-        lax.fori_loop(0, CHUNKS, soften, 0)
+                shares[group, r] = gate / jnp.sum(sums[group, r], axis=1, keepdims=True)
+            return carry
+
+        lax.fori_loop(0, CHUNKS, share, 0)
 
         wait_for(got_v, PEERS - 1, v_here)
         wait_for(got_v, 1, own_v)
@@ -260,13 +302,17 @@
 def body(queries, key_rows, value_rows, noise_levels, gate_table):
     vmem = pl.BlockSpec(memory_space=pltpu.VMEM)
     smem = pl.BlockSpec(memory_space=pltpu.SMEM)
+    hbm = pl.BlockSpec(memory_space=pl.ANY)
+    dma = pltpu.SemaphoreType.DMA
     bf16, f32 = jnp.bfloat16, jnp.float32
     return pl.pallas_call(
         kernel,
         out_shape=jax.ShapeDtypeStruct((ROWS, HEADS, DIM), bf16),
-        in_specs=[vmem, vmem, vmem, smem, smem],
+        in_specs=[hbm, hbm, hbm, smem, smem],
         out_specs=vmem,
-        scratch_shapes=[
+        scratch_shapes=[pltpu.VMEM((ROWS, HEADS, DIM), bf16)] * 3
+        + [
+            dma((3,)),
             pltpu.VMEM((ROWS * HEADS, DIM), f32),
             pltpu.VMEM((HEADS, 2, ROWS, DIM), bf16),
             pltpu.VMEM((HEADS, ROWS, DIM), bf16),
@@ -276,12 +322,12 @@
             pltpu.VMEM((PAIRS, GROUP, SPAN, 1), f32),
             pltpu.VMEM((CHUNKS, GROUP, SPAN, 1), f32),
             pltpu.VMEM((CHUNKS, GROUP, SPAN, 1), f32),
-            pltpu.VMEM((GROUP, SPAN, BLOCK), f32),
+            pltpu.VMEM((CHUNKS, GROUP, SPAN, BLOCK), f32),
             pltpu.VMEM((GROUP, SPAN, DIM), f32),
             pltpu.VMEM((PEERS, ROWS, DIM), bf16),
             pltpu.VMEM((HEADS, ROWS, DIM), bf16),
         ]
-        + [pltpu.SemaphoreType.DMA] * 8,
+        + [dma, dma((CHUNKS,))] + [dma] * 6 + [pltpu.SemaphoreType.REGULAR],
         compiler_params=pltpu.CompilerParams(
             collective_id=0, has_side_effects=True, vmem_limit_bytes=56 << 20
         ),

time: 92.8 us -> 88.1 us (0.949); the launches traced: 91 us -> 87.3 us
  Pallas kernels: 89 us -> 85.2 us
    pallas_call x1, Pallas kernels: 89 us -> 85.2 us  [body(): pl.pallas_call(kernel, out_shape=jax.ShapeDtypeStruct((ROWS, HEADS, DIM),...]
where the time goes in v3:
time: 88.1 us; the launch traced here: 87.3 us
  Pallas kernels  85.2 us (97%)
  local copies, waits for them, and re-layouts  2.06 us (2%)
    pallas_call x1, Pallas kernels, body(): pl.pallas_call(kernel, out_shape=jax.ShapeDtypeStruct((ROWS, HEADS, DIM),...  85.2 us
    unnamed x1, local copies, waits for them, and re-layouts  2.06 us

profile of v3, /device:TPU:248, one launch (start us, length us, event | category | flops | bytes accessed | tf_op | source)
XLA Modules:
  0.0 87.3 jit_solution(3085996628427168397)
XLA Ops:
  0.0 85.2 %shard_map.55 = bf16[64,48,128]{2,1,0:T(8,128)(2,1)} custom-call(bf16[64,48,128]{2,1,0:T(8,128)(2,1)} %queries_hbm.1, bf16[64,48,128]{2,1,0:T(8,128)(2,1)} %key_rows_hbm.1, bf16[64,48,128]{2,1,0:T(8,128)(2,1)} %value_rows_hbm.1, s32[16]{0:T(128)} %noise_levels.1, f32[8,48]{1,0:T(8,128)} %gate_table.1), custom_call_target="tpu_custom_call" | custom-call | tf_op jit(solution)/shard_map/pallas_call | solution.py:308
  85.2 2.1 %copy.7 = bf16[64,48,128]{2,1,0:T(8,128)(2,1)} copy(bf16[64,48,128]{2,1,0:T(8,128)(2,1)} %shard_map.55) | data formatting | bytes 1572864

commit v4 on v3

--- a/solution.py
+++ b/solution.py
@@ -46,9 +46,9 @@
 
 
 def kernel(
-    queries_hbm, key_rows_hbm, value_rows_hbm, noise_levels, gate_table, out,
-    queries, key_rows, value_rows, loaded, wide, send_qk, send_v, got_qk, got_v, weights, peaks, tops, shares, sums, acc, send_o, got_o,
-    qk_sent, qk_here, v_sent, v_here, o_sent, o_here, own_qk, own_v, plane_in,
+    queries_hbm, key_rows_hbm, value_rows_hbm, noise_levels, gate_table, got_o,
+    queries, key_rows, value_rows, loaded, wide, send_qk, send_v, got_qk, got_v, weights, peaks, tops, shares, sums, acc, send_o,
+    qk_sent, qk_here, v_sent, v_here, o_sent, o_here, own_qk, own_v, own_o, plane_in,
 ):
     core = lax.axis_index("video") % 2
     span = lax.axis_index("span")
@@ -149,7 +149,7 @@
     scatter(1, 16, send_qk, got_qk, qk_sent, qk_here.at[y], own_qk)
     loads[2].wait()
     by_head(value_rows, store_v)
-    scatter(0, 16, send_v, got_v, v_sent, v_here, own_v)
+    scatter(0, 16, send_v, got_v, v_sent, v_here.at[y], own_v)
 
     def wait_for(ref, count, semaphore):
         part = ref.at[pl.ds(0, count)]
@@ -225,37 +225,24 @@
             for r in range(GROUP):
                 gate = gate_table[noise_levels[group * GROUP + r], my_head]
                 shares[group, r] = gate / jnp.sum(sums[group, r], axis=1, keepdims=True)
+                acc[group, r] = jnp.zeros((SPAN, DIM), jnp.float32)
             return carry
 
         lax.fori_loop(0, CHUNKS, share, 0)
 
-        wait_for(got_v, PEERS - 1, v_here)
-        wait_for(got_v, 1, own_v)
-
-        def gather(step, carry):
-            group = step
-
-            def term(chunk, spans, r):
-                pair = pair_at(group, chunk)
-                rescale = jnp.exp2((peaks[pair, r] - tops[group, r]) * SCALE)
-                return rescale * jnp.dot(
-                    weights[pair, r, :, 0 : spans * SPAN],
-                    values_of(chunk, spans),
-                    preferred_element_type=jnp.float32,
-                )
-
-            for r in range(GROUP):
-                acc[r] = term(group, r + 1, r)
-
-            def earlier(chunk, carry):
-                for r in range(GROUP):
-                    acc[r] += term(chunk, GROUP, r)
-                return carry
-
-            lax.fori_loop(0, group, earlier, 0)
+        def add_term(group, chunk, spans, r):
+            pair = pair_at(group, chunk)
+            rescale = jnp.exp2((peaks[pair, r] - tops[group, r]) * SCALE)
+            acc[group, r] += rescale * jnp.dot(
+                weights[pair, r, :, 0 : spans * SPAN],
+                values_of(chunk, spans),
+                preferred_element_type=jnp.float32,
+            )
+
+        def give_back(group):
             for r in range(GROUP):
                 i = group * GROUP + r
-                result = (acc[r] * shares[group, r]).astype(jnp.bfloat16)
+                result = (acc[group, r] * shares[group, r]).astype(jnp.bfloat16)
                 send_o[pl.ds(i * QUARTERS, QUARTERS)] = result.reshape(QUARTERS, ROWS, DIM)
                 for quarter in range(QUARTERS):
                     piece = i * QUARTERS + quarter
@@ -274,12 +261,43 @@
 
                     @pl.when(mine)
                     def _():
-                        got_o[my_head] = send_o[piece]
-
+                        pltpu.make_async_copy(send_o.at[piece], got_o.at[my_head], own_o).start()
+
+        def gather(step, carry):
+            row = row_of(step)
+
+            @pl.when(step == 0)
+            def _():
+                wait_for(got_v, 15, v_here.at[row])
+                wait_for(got_v, 1, own_v)
+
+            @pl.when(step > 0)
+            def _():
+                wait_for(got_v, 16, v_here.at[row])
+
+            def into(group, carry):
+                @pl.when(group == row)
+                def _():
+                    for r in range(GROUP):
+                        add_term(group, group, r + 1, r)
+
+                @pl.when(group > row)
+                def _():
+                    for r in range(GROUP):
+                        add_term(group, row, GROUP, r)
+
+                @pl.when(step == jnp.where(group <= y, y, CHUNKS - 1))
+                def _():
+                    give_back(group)
+
+                return carry
+
+            lax.fori_loop(row, CHUNKS, into, 0)
             return carry
 
         lax.fori_loop(0, CHUNKS, gather, 0)
         wait_for(got_o, HEADS - 1, o_here)
+        wait_for(got_o, 1, own_o)
         wait_for(send_qk, HEADS - 1, qk_sent)
         wait_for(send_v, HEADS - 1, v_sent)
         wait_for(send_o, PEERS - 1, o_sent)
@@ -290,26 +308,17 @@
         wait_for(send_qk, HEADS, qk_sent)
         wait_for(send_v, HEADS, v_sent)
 
-    wide[...] = got_o[...].reshape(HEADS * ROWS, DIM).astype(jnp.float32)
-
-    def token(t, carry):
-        out[t] = wide[pl.ds(t, HEADS, stride=ROWS), :].astype(jnp.bfloat16)
-        return carry
-
-    lax.fori_loop(0, ROWS, token, 0)
-
 
 def body(queries, key_rows, value_rows, noise_levels, gate_table):
-    vmem = pl.BlockSpec(memory_space=pltpu.VMEM)
     smem = pl.BlockSpec(memory_space=pltpu.SMEM)
     hbm = pl.BlockSpec(memory_space=pl.ANY)
     dma = pltpu.SemaphoreType.DMA
     bf16, f32 = jnp.bfloat16, jnp.float32
-    return pl.pallas_call(
+    by_head = pl.pallas_call(
         kernel,
-        out_shape=jax.ShapeDtypeStruct((ROWS, HEADS, DIM), bf16),
+        out_shape=jax.ShapeDtypeStruct((HEADS, ROWS, DIM), bf16),
         in_specs=[hbm, hbm, hbm, smem, smem],
-        out_specs=vmem,
+        out_specs=hbm,
         scratch_shapes=[pltpu.VMEM((ROWS, HEADS, DIM), bf16)] * 3
         + [
             dma((3,)),
@@ -323,15 +332,15 @@
             pltpu.VMEM((CHUNKS, GROUP, SPAN, 1), f32),
             pltpu.VMEM((CHUNKS, GROUP, SPAN, 1), f32),
             pltpu.VMEM((CHUNKS, GROUP, SPAN, BLOCK), f32),
-            pltpu.VMEM((GROUP, SPAN, DIM), f32),
+            pltpu.VMEM((CHUNKS, GROUP, SPAN, DIM), f32),
             pltpu.VMEM((PEERS, ROWS, DIM), bf16),
-            pltpu.VMEM((HEADS, ROWS, DIM), bf16),
         ]
-        + [dma, dma((CHUNKS,))] + [dma] * 6 + [pltpu.SemaphoreType.REGULAR],
+        + [dma, dma((CHUNKS,))] * 2 + [dma] * 5 + [pltpu.SemaphoreType.REGULAR],
         compiler_params=pltpu.CompilerParams(
             collective_id=0, has_side_effects=True, vmem_limit_bytes=56 << 20
         ),
     )(queries, key_rows, value_rows, noise_levels, gate_table)
+    return jnp.swapaxes(by_head, 0, 1)
 
 
 def solution(mesh):

time: 88.1 us -> 85.4 us (0.969)
  Pallas kernels: 85.2 us -> 82.3 us
    pallas_call x1, Pallas kernels: 85.2 us -> 82.3 us  [body(): pl.pallas_call(kernel, out_shape=jax.ShapeDtypeStruct((HEADS, ROWS, DIM),...]
    transpose x0 -> x1, local copies, waits for them, and re-layouts: none -> 2.52 us  [body(): return jnp.swapaxes(by_head, 0, 1)]
    unnamed x1 -> x0, local copies, waits for them, and re-layouts: 2.06 us -> none
where the time goes in v4:
time: 85.4 us; the launch traced here: 84.8 us
  Pallas kernels  82.3 us (96%)
  local copies, waits for them, and re-layouts  2.52 us (3%)
    pallas_call x1, Pallas kernels, body(): pl.pallas_call(kernel, out_shape=jax.ShapeDtypeStruct((HEADS, ROWS, DIM),...  82.3 us
    transpose x1, local copies, waits for them, and re-layouts, body(): return jnp.swapaxes(by_head, 0, 1)  2.52 us

profile of v4, /device:TPU:248, one launch (start us, length us, event | category | flops | bytes accessed | tf_op | source)
XLA Modules:
  0.0 84.8 jit_solution(12882702188797584583)
XLA Ops:
  0.0 82.3 %shard_map.55 = bf16[48,64,128]{2,1,0:T(8,128)(2,1)} custom-call(bf16[64,48,128]{2,1,0:T(8,128)(2,1)} %queries_hbm.1, bf16[64,48,128]{2,1,0:T(8,128)(2,1)} %key_rows_hbm.1, bf16[64,48,128]{2,1,0:T(8,128)(2,1)} %value_rows_hbm.1, s32[16]{0:T(128)} %noise_levels.1, f32[8,48]{1,0:T(8,128)} %gate_table.1), custom_call_target="tpu_custom_call" | custom-call | tf_op jit(solution)/shard_map/pallas_call | solution.py:317
  82.3 2.5 %copy.6 = bf16[64,48,128]{2,1,0:T(8,128)(2,1)} copy(bf16[64,48,128]{2,0,1:T(8,128)(2,1)} %bitcast.1) | data formatting | bytes 1572864 | tf_op jit(solution)/shard_map/transpose | solution.py:343

commit v5 on v4

--- a/solution.py
+++ b/solution.py
@@ -47,7 +47,7 @@
 
 def kernel(
     queries_hbm, key_rows_hbm, value_rows_hbm, noise_levels, gate_table, got_o,
-    queries, key_rows, value_rows, loaded, wide, send_qk, send_v, got_qk, got_v, weights, peaks, tops, shares, sums, acc, send_o,
+    queries, key_rows, value_rows, loaded, wide_q, wide_k, wide_v, send_qk, send_v, got_qk, got_v, weights, peaks, tops, shares, sums, acc, send_o,
     qk_sent, qk_here, v_sent, v_here, o_sent, o_here, own_qk, own_v, own_o, plane_in,
 ):
     core = lax.axis_index("video") % 2
@@ -58,8 +58,14 @@
     me = span * QUARTERS + x
 
     def place(column_x, column_y, j):
-        z_at = (0, 1 + core, 3)[j]
+        z_at = (j * 3) // 2 + jnp.where(j == 1, core, 0)
         return (column_y * 4 + column_x) * 3 + j, column_y * 4 + z_at, column_x
+
+    j_far = jnp.where(z < 2, 2, 0)
+    j_near = jnp.where(z == 0, 0, jnp.where(z == 3, 2, 1))
+
+    def by_distance(turn):
+        return jnp.where(turn == 0, j_far, jnp.where(turn == 2, j_near, 3 - j_far - j_near))
 
     active = (z == 0) | (z == 3) | (z == 1 + core)
     j_mine = jnp.where(z == 0, 0, jnp.where(z == 3, 2, 1))
@@ -92,68 +98,82 @@
     for i in range(1, 16):
         signal(barrier, lax.rem(y + i // 4, 4) * 4 + z, lax.rem(x + i % 4, 4))
 
-    def by_head(ref, store):
+    def widen(ref, wide):
         wide[...] = ref[...].reshape(ROWS * HEADS, DIM).astype(jnp.float32)
 
-        def one(h, carry):
-            store(h, wide[pl.ds(h, ROWS, stride=HEADS), :].astype(jnp.bfloat16))
-            return carry
-
-        lax.fori_loop(0, HEADS, one, 0)
-
-    def store_q(h, rows):
-        send_qk[h, 0] = rows
-
-    def store_k(h, rows):
-        send_qk[h, 1] = rows
-
-    def store_v(h, rows):
-        send_v[h] = rows
+    def head_of(wide, head):
+        return wide[pl.ds(head, ROWS, stride=HEADS), :].astype(jnp.bfloat16)
+
+    def lay_out_qk(head):
+        send_qk[head, 0] = head_of(wide_q, head)
+        send_qk[head, 1] = head_of(wide_k, head)
+
+    def lay_out_v(head):
+        send_v[head] = head_of(wide_v, head)
 
     loads[0].wait()
-    by_head(queries, store_q)
+    widen(queries, wide_q)
     loads[1].wait()
-    by_head(key_rows, store_k)
+    widen(key_rows, wide_k)
     pl.semaphore_wait(barrier, 3 + 15)
     greet_column(plane_in)
 
-    def scatter(first, last, source, target, sent, here, own):
-        def column(k, carry):
-            column_x = lax.rem(x + k % 4, 4)
-            column_y = lax.rem(y + k // 4, 4)
-            for j in range(3):
-                head, to_span, to_x = place(column_x, column_y, j)
-                mine = (to_span == span) & (to_x == x)
-
-                @pl.when(jnp.logical_not(mine))
-                def _():
-                    pltpu.make_async_remote_copy(
-                        source.at[head],
-                        target.at[me],
-                        sent,
-                        here,
-                        device_id={"span": to_span, "head": to_x},
-                        device_id_type=MESH,
-                    ).start()
-
-                @pl.when(mine)
-                def _():
-                    pltpu.make_async_copy(source.at[head], target.at[me], own).start()
-
-            return carry
-
-        lax.fori_loop(first, last, column, 0)
-
-    scatter(0, 1, send_qk, got_qk, qk_sent, qk_here.at[y], own_qk)
-    pl.semaphore_wait(plane_in, 3)
-    scatter(1, 16, send_qk, got_qk, qk_sent, qk_here.at[y], own_qk)
-    loads[2].wait()
-    by_head(value_rows, store_v)
-    scatter(0, 16, send_v, got_v, v_sent, v_here.at[y], own_v)
+    def send_one(k, turn, lay_out, source, target, sent, here, own):
+        column_x = lax.rem(x + k % 4, 4)
+        column_y = lax.rem(y + k // 4, 4)
+        head, to_span, to_x = place(column_x, column_y, by_distance(turn))
+        lay_out(head)
+        mine = (to_span == span) & (to_x == x)
+
+        @pl.when(jnp.logical_not(mine))
+        def _():
+            pltpu.make_async_remote_copy(
+                source.at[head],
+                target.at[me],
+                sent,
+                here,
+                device_id={"span": to_span, "head": to_x},
+                device_id_type=MESH,
+            ).start()
+
+        @pl.when(mine)
+        def _():
+            pltpu.make_async_copy(source.at[head], target.at[me], own).start()
+
+    def scatter_column(*way):
+        def one(turn, carry):
+            send_one(0, turn, *way)
+            return carry
+
+        lax.fori_loop(0, 3, one, 0)
+
+    def scatter_rest(*way):
+        def one(n, carry):
+            k = (n // 12) * 4 + n % 4
+            turn = 2 - (n % 12) // 4
+
+            @pl.when(k > 0)
+            def _():
+                send_one(k, turn, *way)
+
+            return carry
+
+        lax.fori_loop(0, HEADS, one, 0)
+
+    way_qk = (lay_out_qk, send_qk, got_qk, qk_sent, qk_here.at[y], own_qk)
+    way_v = (lay_out_v, send_v, got_v, v_sent, v_here.at[y], own_v)
 
     def wait_for(ref, count, semaphore):
         part = ref.at[pl.ds(0, count)]
         pltpu.make_async_copy(part, part, semaphore).wait()
+
+    scatter_column(*way_qk)
+    loads[2].wait()
+    widen(value_rows, wide_v)
+    scatter_column(*way_v)
+    pl.semaphore_wait(plane_in, 3)
+    scatter_rest(*way_qk)
+    scatter_rest(*way_v)
 
     @pl.when(active)
     def _():
@@ -322,6 +342,8 @@
         scratch_shapes=[pltpu.VMEM((ROWS, HEADS, DIM), bf16)] * 3
         + [
             dma((3,)),
+            pltpu.VMEM((ROWS * HEADS, DIM), f32),
+            pltpu.VMEM((ROWS * HEADS, DIM), f32),
             pltpu.VMEM((ROWS * HEADS, DIM), f32),
             pltpu.VMEM((HEADS, 2, ROWS, DIM), bf16),
             pltpu.VMEM((HEADS, ROWS, DIM), bf16),

time: 85.4 us -> 84.2 us (0.986)
  Pallas kernels: 82.3 us -> 80.3 us
    pallas_call x1, Pallas kernels: 82.3 us -> 80.3 us  [body(): pl.pallas_call(kernel, out_shape=jax.ShapeDtypeStruct((HEADS, ROWS, DIM),...]
where the time goes in v5:
time: 84.2 us; the launch traced here: 82.9 us
  Pallas kernels  80.3 us (95%)
  local copies, waits for them, and re-layouts  2.52 us (3%)
    pallas_call x1, Pallas kernels, body(): pl.pallas_call(kernel, out_shape=jax.ShapeDtypeStruct((HEADS, ROWS, DIM),...  80.3 us
    transpose x1, local copies, waits for them, and re-layouts, body(): return jnp.swapaxes(by_head, 0, 1)  2.52 us

profile of v5, /device:TPU:248, one launch (start us, length us, event | category | flops | bytes accessed | tf_op | source)
XLA Modules:
  0.0 82.9 jit_solution(6884768771065971323)
XLA Ops:
  0.0 80.3 %shard_map.55 = bf16[48,64,128]{2,1,0:T(8,128)(2,1)} custom-call(bf16[64,48,128]{2,1,0:T(8,128)(2,1)} %queries_hbm.1, bf16[64,48,128]{2,1,0:T(8,128)(2,1)} %key_rows_hbm.1, bf16[64,48,128]{2,1,0:T(8,128)(2,1)} %value_rows_hbm.1, s32[16]{0:T(128)} %noise_levels.1, f32[8,48]{1,0:T(8,128)} %gate_table.1), custom_call_target="tpu_custom_call" | custom-call | tf_op jit(solution)/shard_map/pallas_call | solution.py:337
  80.3 2.5 %copy.6 = bf16[64,48,128]{2,1,0:T(8,128)(2,1)} copy(bf16[64,48,128]{2,0,1:T(8,128)(2,1)} %bitcast.1) | data formatting | bytes 1572864 | tf_op jit(solution)/shard_map/transpose | solution.py:365

commit v6 on v5

--- a/solution.py
+++ b/solution.py
@@ -46,8 +46,8 @@
 
 
 def kernel(
-    queries_hbm, key_rows_hbm, value_rows_hbm, noise_levels, gate_table, got_o,
-    queries, key_rows, value_rows, loaded, wide_q, wide_k, wide_v, send_qk, send_v, got_qk, got_v, weights, peaks, tops, shares, sums, acc, send_o,
+    queries_hbm, key_rows_hbm, value_rows_hbm, noise_levels_hbm, gate_table_hbm, got_o,
+    queries, key_rows, value_rows, noise_levels, gate_table, loaded, wide_q, wide_k, wide_v, send_qk, send_v, got_qk, got_v, weights, peaks, tops, shares, sums, acc, send_o,
     qk_sent, qk_here, v_sent, v_here, o_sent, o_here, own_qk, own_v, own_o, plane_in,
 ):
     core = lax.axis_index("video") % 2
@@ -74,7 +74,13 @@
     loads = [
         pltpu.make_async_copy(source, target, loaded.at[n])
         for n, (source, target) in enumerate(
-            [(queries_hbm, queries), (key_rows_hbm, key_rows), (value_rows_hbm, value_rows)]
+            [
+                (queries_hbm, queries),
+                (key_rows_hbm, key_rows),
+                (value_rows_hbm, value_rows),
+                (noise_levels_hbm, noise_levels),
+                (gate_table_hbm, gate_table),
+            ]
         )
     ]
     for load in loads:
@@ -147,10 +153,9 @@
 
         lax.fori_loop(0, 3, one, 0)
 
-    def scatter_rest(*way):
+    def scatter_rest(order, *way):
         def one(n, carry):
-            k = (n // 12) * 4 + n % 4
-            turn = 2 - (n % 12) // 4
+            k, turn = order(n)
 
             @pl.when(k > 0)
             def _():
@@ -168,12 +173,19 @@
         pltpu.make_async_copy(part, part, semaphore).wait()
 
     scatter_column(*way_qk)
-    loads[2].wait()
+    for load in loads[2:]:
+        load.wait()
     widen(value_rows, wide_v)
     scatter_column(*way_v)
     pl.semaphore_wait(plane_in, 3)
-    scatter_rest(*way_qk)
-    scatter_rest(*way_v)
+    def rows_near(n):
+        return (n // 12) * 4 + n % 4, 2 - (n % 12) // 4
+
+    def rows_v(n):
+        return n % 16, 2 - n // 16
+
+    scatter_rest(rows_near, *way_qk)
+    scatter_rest(rows_v, *way_v)
 
     @pl.when(active)
     def _():
@@ -329,19 +341,21 @@
         wait_for(send_v, HEADS, v_sent)
 
 
-def body(queries, key_rows, value_rows, noise_levels, gate_table):
-    smem = pl.BlockSpec(memory_space=pltpu.SMEM)
-    hbm = pl.BlockSpec(memory_space=pl.ANY)
+def body(*operands):
+    hbm = pl.BlockSpec(memory_space=pltpu.HBM)
+    anywhere = pl.BlockSpec(memory_space=pl.ANY)
     dma = pltpu.SemaphoreType.DMA
     bf16, f32 = jnp.bfloat16, jnp.float32
     by_head = pl.pallas_call(
         kernel,
         out_shape=jax.ShapeDtypeStruct((HEADS, ROWS, DIM), bf16),
-        in_specs=[hbm, hbm, hbm, smem, smem],
-        out_specs=hbm,
+        in_specs=[hbm] * 5,
+        out_specs=anywhere,
         scratch_shapes=[pltpu.VMEM((ROWS, HEADS, DIM), bf16)] * 3
         + [
-            dma((3,)),
+            pltpu.SMEM((SPANS,), jnp.int32),
+            pltpu.SMEM((8, HEADS), f32),
+            dma((5,)),
             pltpu.VMEM((ROWS * HEADS, DIM), f32),
             pltpu.VMEM((ROWS * HEADS, DIM), f32),
             pltpu.VMEM((ROWS * HEADS, DIM), f32),
@@ -359,9 +373,9 @@
         ]
         + [dma, dma((CHUNKS,))] * 2 + [dma] * 5 + [pltpu.SemaphoreType.REGULAR],
         compiler_params=pltpu.CompilerParams(
-            collective_id=0, has_side_effects=True, vmem_limit_bytes=56 << 20
+            collective_id=0, has_side_effects=True, vmem_limit_bytes=53 << 20
         ),
-    )(queries, key_rows, value_rows, noise_levels, gate_table)
+    )(*[pltpu.with_memory_space_constraint(operand, pltpu.HBM) for operand in operands])
     return jnp.swapaxes(by_head, 0, 1)
 
 

time: 84.2 us -> 81.2 us (0.964); the launches traced: 82.9 us -> 80.8 us
  local copies, waits for them, and re-layouts: 2.52 us -> 1.39 us
  Pallas kernels: 80.3 us -> 79.4 us
    transpose x1, local copies, waits for them, and re-layouts: 2.52 us -> 1.39 us  [body(): return jnp.swapaxes(by_head, 0, 1)]
    pallas_call x1, Pallas kernels: 80.3 us -> 79.4 us  [body(): pl.pallas_call(kernel, out_shape=jax.ShapeDtypeStruct((HEADS, ROWS, DIM),...]
where the time goes in v6:
time: 81.2 us; the launch traced here: 80.8 us
  Pallas kernels  79.4 us (98%)
  local copies, waits for them, and re-layouts  1.39 us (2%)
    pallas_call x1, Pallas kernels, body(): pl.pallas_call(kernel, out_shape=jax.ShapeDtypeStruct((HEADS, ROWS, DIM),...  79.4 us

profile of v6, /device:TPU:248, one launch (start us, length us, event | category | flops | bytes accessed | tf_op | source)
XLA Modules:
  0.0 80.8 jit_solution(8957569456969764356)
XLA Ops:
  0.0 79.4 %shard_map.55 = bf16[48,64,128]{2,1,0:T(8,128)(2,1)S(1)} custom-call(bf16[64,48,128]{2,1,0:T(8,128)(2,1)} %queries_hbm.1, bf16[64,48,128]{2,1,0:T(8,128)(2,1)} %key_rows_hbm.1, bf16[64,48,128]{2,1,0:T(8,128)(2,1)} %value_rows_hbm.1, s32[16]{0:T(128)} %noise_levels_hbm.1, f32[8,48]{1,0:T(8,128)} %gate_table_hbm.1), custom_call_target="tpu_custom_call" | custom-call | tf_op jit(solution)/shard_map/pallas_call | solution.py:349
  79.4 1.4 %copy.6 = bf16[64,48,128]{2,1,0:T(8,128)(2,1)} copy(bf16[64,48,128]{2,0,1:T(8,128)(2,1)S(1)} %bitcast.1) | data formatting | bytes 1572864 | tf_op jit(solution)/shard_map/transpose | solution.py:379

commit v7 on v6

--- a/solution.py
+++ b/solution.py
@@ -124,9 +124,9 @@
     pl.semaphore_wait(barrier, 3 + 15)
     greet_column(plane_in)
 
-    def send_one(k, turn, lay_out, source, target, sent, here, own):
+    def send_one(k, turn, stride_y, lay_out, source, target, sent, here, own):
         column_x = lax.rem(x + k % 4, 4)
-        column_y = lax.rem(y + k // 4, 4)
+        column_y = lax.rem(y + stride_y * (k // 4), 4)
         head, to_span, to_x = place(column_x, column_y, by_distance(turn))
         lay_out(head)
         mine = (to_span == span) & (to_x == x)
@@ -165,8 +165,8 @@
 
         lax.fori_loop(0, HEADS, one, 0)
 
-    way_qk = (lay_out_qk, send_qk, got_qk, qk_sent, qk_here.at[y], own_qk)
-    way_v = (lay_out_v, send_v, got_v, v_sent, v_here.at[y], own_v)
+    way_qk = (3, lay_out_qk, send_qk, got_qk, qk_sent, qk_here.at[y], own_qk)
+    way_v = (1, lay_out_v, send_v, got_v, v_sent, v_here.at[y], own_v)
 
     def wait_for(ref, count, semaphore):
         part = ref.at[pl.ds(0, count)]
@@ -227,7 +227,7 @@
                 tops[group, r] = top
 
         def row_of(step):
-            return lax.rem(y + CHUNKS - step, CHUNKS)
+            return lax.rem(y + step, CHUNKS)
 
         def soften(step, carry):
             row = row_of(step)
@@ -296,7 +296,7 @@
                         pltpu.make_async_copy(send_o.at[piece], got_o.at[my_head], own_o).start()
 
         def gather(step, carry):
-            row = row_of(step)
+            row = lax.rem(y + CHUNKS - step, CHUNKS)
 
             @pl.when(step == 0)
             def _():

time: 81.2 us -> 81 us (level)
  no operation moved by 1% of the time
where the time goes in v7:
time: 81 us; the launch traced here: 80.8 us
  Pallas kernels  79.4 us (98%)
  local copies, waits for them, and re-layouts  1.39 us (2%)
    pallas_call x1, Pallas kernels, body(): pl.pallas_call(kernel, out_shape=jax.ShapeDtypeStruct((HEADS, ROWS, DIM),...  79.4 us

profile of v7, /device:TPU:248, one launch (start us, length us, event | category | flops | bytes accessed | tf_op | source)
XLA Modules:
  0.0 80.8 jit_solution(11872274349156046425)
XLA Ops:
  0.0 79.4 %shard_map.55 = bf16[48,64,128]{2,1,0:T(8,128)(2,1)S(1)} custom-call(bf16[64,48,128]{2,1,0:T(8,128)(2,1)} %queries_hbm.1, bf16[64,48,128]{2,1,0:T(8,128)(2,1)} %key_rows_hbm.1, bf16[64,48,128]{2,1,0:T(8,128)(2,1)} %value_rows_hbm.1, s32[16]{0:T(128)} %noise_levels_hbm.1, f32[8,48]{1,0:T(8,128)} %gate_table_hbm.1), custom_call_target="tpu_custom_call" | custom-call | tf_op jit(solution)/shard_map/pallas_call | solution.py:349
  79.4 1.4 %copy.6 = bf16[64,48,128]{2,1,0:T(8,128)(2,1)} copy(bf16[64,48,128]{2,0,1:T(8,128)(2,1)S(1)} %bitcast.1) | data formatting | bytes 1572864 | tf_op jit(solution)/shard_map/transpose | solution.py:379

commit v8 on v7

--- a/solution.py
+++ b/solution.py
@@ -125,7 +125,9 @@
     greet_column(plane_in)
 
     def send_one(k, turn, stride_y, lay_out, source, target, sent, here, own):
-        column_x = lax.rem(x + k % 4, 4)
+        k_x = k % 4
+        k_x = k_x + jnp.where(k_x == 2, 1, 0) - jnp.where(k_x == 3, 1, 0)
+        column_x = lax.rem(x + k_x, 4)
         column_y = lax.rem(y + stride_y * (k // 4), 4)
         head, to_span, to_x = place(column_x, column_y, by_distance(turn))
         lay_out(head)

time: 81 us -> 81.5 us (level)
  no operation moved by 1% of the time
where the time goes in v8:
time: 81.5 us; the launch traced here: 80.9 us
  Pallas kernels  79.5 us (98%)
  local copies, waits for them, and re-layouts  1.39 us (2%)
    pallas_call x1, Pallas kernels, body(): pl.pallas_call(kernel, out_shape=jax.ShapeDtypeStruct((HEADS, ROWS, DIM),...  79.5 us

profile of v8, /device:TPU:248, one launch (start us, length us, event | category | flops | bytes accessed | tf_op | source)
XLA Modules:
  0.0 80.9 jit_solution(15466866764397446273)
XLA Ops:
  0.0 79.5 %shard_map.55 = bf16[48,64,128]{2,1,0:T(8,128)(2,1)S(1)} custom-call(bf16[64,48,128]{2,1,0:T(8,128)(2,1)} %queries_hbm.1, bf16[64,48,128]{2,1,0:T(8,128)(2,1)} %key_rows_hbm.1, bf16[64,48,128]{2,1,0:T(8,128)(2,1)} %value_rows_hbm.1, s32[16]{0:T(128)} %noise_levels_hbm.1, f32[8,48]{1,0:T(8,128)} %gate_table_hbm.1), custom_call_target="tpu_custom_call" | custom-call | tf_op jit(solution)/shard_map/pallas_call | solution.py:351
  79.5 1.4 %copy.6 = bf16[64,48,128]{2,1,0:T(8,128)(2,1)} copy(bf16[64,48,128]{2,0,1:T(8,128)(2,1)S(1)} %bitcast.1) | data formatting | bytes 1572864 | tf_op jit(solution)/shard_map/transpose | solution.py:381
